TPU v7x, 32 devices: a whole 2x2x4 slice. The times are simulated.
32 devices in a mesh: cluster: 2 (over x), sub: 16 (over z, y, core).
Axes of the slice: x: 2, y: 2, z: 4, core: 2. Of those that a mesh axis runs over, the one named last changes fastest.
Arguments:
- load_terms: float32 [32, 128, 1536], P(('cluster', 'sub')), may hold values from -60 to 60
- dual_operator: bfloat16 [32, 1536, 1536], P(('cluster', 'sub')), may hold values from -2 to 16, as said below
- dirichlet: bfloat16 [32, 1536, 1536], P(('cluster', 'sub')), may hold values from -2 to 16, as said below
- corner_coupling: bfloat16 [32, 1536, 24], P(('cluster', 'sub')), may hold values from -0.25 to 0.25
- coarse_inverse: float32 [96, 96], P(('cluster', 'sub')), may hold values from -2 to 4, as said below
- face_map: int32 [32, 6, 256], P(('cluster', 'sub')), may hold values from 0 to 255, as said below
- face_live: int32 [32, 6], P(('cluster', 'sub')), may hold values from 0 to 1, as said below
- corner_ids: int32 [32, 8], P(('cluster', 'sub')), may hold values from 0 to 31, as said below
Outputs:
- multipliers: float32 [32, 128, 1536], P(('cluster', 'sub'))
- residual: float32 [32, 128, 1536], P(('cluster', 'sub'))
Inputs may be any that keep to these rules, and one draw needn't show every extreme that they name: face_map[d, f] is a permutation of the slots of a face; the maps of the two sides of a face pair are inverse to each other. `face_live`: equal on the two sides of a face pair. `corner_ids`: the eight corners of a subdomain are the lattice vertices (c + a, s + b + 4 * e) for a, b, e in 0 and 1, taken modulo 2 and 16; each vertex has one number and is shared by eight subdomains. `dual_operator`: each subdomain's matrix is symmetric and positive definite. `dirichlet`: each subdomain's matrix is symmetric and positive definite. `coarse_inverse`: symmetric and positive definite.
All inputs are finite; a program needn't handle non-finite values.
Results may differ from a plain program's by a relative error of at most 0.0099.
Values sent between devices are 32-bit elements; how exact they have to be, the bound alone decides.
No kernel may reach another device: no remote copies, remote signals or barrier semaphores. Data moves between devices by JAX's collectives and lax.ppermute only.
A program may use at most 128 MiB of HBM per device.

v0:
```python
import jax
import jax.numpy as jnp
from jax import lax
from jax.sharding import PartitionSpec as P

ITERS = 2
STRIDE = 4


def padded(block, sides, width):
    for axis, dim in sides:
        count = lax.axis_size(axis)
        forward = [(i, i + 1) for i in range(count - 1)]
        forward.append((count - 1, 0))
        backward = [(target, source) for source, target in forward]
        low = lax.ppermute(
            lax.slice_in_dim(block, block.shape[dim] - width, None, axis=dim), axis, forward
        )
        high = lax.ppermute(lax.slice_in_dim(block, 0, width, axis=dim), axis, backward)
        block = jnp.concatenate([low, block, high], axis=dim)
    return block


def passed_along(value, axis, steps):
    count = lax.axis_size(axis)
    pairs = [(source, (source + steps) % count) for source in range(count)]
    return lax.ppermute(value, axis, pairs)


def local(
    load_terms,
    dual_operator,
    dirichlet,
    corner_coupling,
    coarse_inverse,
    face_map,
    face_live,
    corner_ids,
):
    local_loads = load_terms[0]
    operator_local = dual_operator[0]
    precond_local = dirichlet[0]
    coupling = corner_coupling[0]
    slot_maps = face_map[0]
    live_faces = face_live[0].astype(jnp.float32)
    corners = corner_ids[0]
    load_count = local_loads.shape[0]
    dual_size = local_loads.shape[1]
    face_size = dual_size // 6
    coarse_size = coarse_inverse.shape[1]
    coarse_index = (3 * corners[:, None] + jnp.arange(3, dtype=jnp.int32)[None, :]).reshape(-1)
    spread = (coarse_index[:, None] == jnp.arange(coarse_size, dtype=jnp.int32)[None, :]).astype(
        jnp.float32
    )

    def assemble(local_sum):
        face_parts = local_sum.reshape(load_count, 6, face_size)
        slab_pair = padded(jnp.stack([face_parts[:, 0], face_parts[:, 1]]), (("cluster", 0),), 1)
        row_pair = padded(jnp.stack([face_parts[:, 2], face_parts[:, 3]]), (("sub", 0),), 1)
        column_pair = []
        for source_face, shift_step in ((5, STRIDE), (4, -STRIDE)):
            column_pair.append(passed_along(face_parts[:, source_face], "sub", shift_step))
        received = [
            slab_pair[0],
            slab_pair[3],
            row_pair[0],
            row_pair[3],
            column_pair[0],
            column_pair[1],
        ]
        pieces = []
        for face_index in range(6):
            permuted = jnp.take(received[face_index], slot_maps[face_index], axis=1)
            pieces.append((face_parts[:, face_index] + permuted) * live_faces[face_index])
        return jnp.concatenate(pieces, axis=1)

    def precond_with_product(vector):
        local_term = jnp.dot(
            vector.astype(jnp.bfloat16), precond_local, preferred_element_type=jnp.float32
        )
        precond = assemble(local_term)
        product = 0.5 * lax.psum(jnp.sum(vector * precond, axis=1), ("cluster", "sub"))
        return (precond, product)

    right_side = assemble(local_loads)
    multipliers = jnp.zeros_like(right_side)
    residual = right_side
    precond, residual_dot = precond_with_product(residual)
    direction = precond
    for iteration in range(ITERS):
        rounded = direction.astype(jnp.bfloat16)
        direct = jnp.dot(rounded, operator_local, preferred_element_type=jnp.float32)
        corner_terms = jnp.dot(rounded, coupling, preferred_element_type=jnp.float32)
        coarse_local = jnp.dot(corner_terms, spread, precision=lax.Precision.HIGHEST)
        local_curve = jnp.sum(direction * direct, axis=1)
        apply_coarse_load, curve_total = lax.psum((coarse_local, local_curve), ("cluster", "sub"))
        own_values = jnp.dot(apply_coarse_load, coarse_inverse.T, precision=lax.Precision.HIGHEST)
        solution = lax.all_gather(own_values, ("cluster", "sub"), axis=1, tiled=True)
        corner_values = jnp.dot(solution, spread.T, precision=lax.Precision.HIGHEST).astype(
            jnp.bfloat16
        )
        back = lax.dot_general(
            corner_values, coupling, (((1,), (1,)), ((), ())), preferred_element_type=jnp.float32
        )
        dual_image = assemble(direct + back)
        curvature = curve_total + jnp.sum(apply_coarse_load * solution, axis=1)
        dual_image, curvature = (dual_image, curvature)
        step_size = residual_dot / curvature
        multipliers = multipliers + step_size[:, None] * direction
        residual = residual - step_size[:, None] * dual_image
        if iteration + 1 < ITERS:
            precond, residual_new = precond_with_product(residual)
            direction = precond + (residual_new / residual_dot)[:, None] * direction
            residual_dot = residual_new
    return (multipliers[None], residual[None])


def solution(mesh):
    placed = (
        P(("cluster", "sub"), None, None),
        P(("cluster", "sub"), None, None),
        P(("cluster", "sub"), None, None),
        P(("cluster", "sub"), None, None),
        P(("cluster", "sub"), None),
        P(("cluster", "sub"), None, None),
        P(("cluster", "sub"), None),
        P(("cluster", "sub"), None),
    )
    return jax.shard_map(
        local,
        mesh=mesh,
        in_specs=placed,
        out_specs=(P(("cluster", "sub"), None, None), P(("cluster", "sub"), None, None)),
        check_vma=False,
    )
```

profile of v0, /device:TPU:0, one launch (start us, length us, event | category | flops | bytes accessed | tf_op | source)
XLA Modules:
  0.0 432.1 jit_solution(1258101771140866283)
XLA Ops:
  2.3 3.0 collective-permute-start
  5.8 4.5 %collective-permute-start.3 = (f32[1,128,256]{2,1,0:T(8,128)S(1)}, f32[1,128,256]{2,1,0:T(8,128)S(1)}, u32[]{:S(2)}, u32[]{:S(2)}) collective-permute-start(f32[1,128,256]{2,1,0:T(8,128)S(1)} %bitcast.561), channel_id=1, source_target_pairs={{1,0},{2,1},{3,2},{4,3},{5,4},{6,5},{7,6},{8,7},{9,8},{10,9},{11,1... | collective-permute-start | bytes 393224 | tf_op jit(solution)/shard_map/ppermute | solution.py:19
  12.5 3.6 collective-permute-start.5
  16.1 6.6 %copy.173 = bf16[1,1536,1536]{1,2,0:T(8,128)(2,1)} copy(bf16[1,1536,1536]{2,1,0:T(8,128)(2,1)} %param.12) | data formatting | bytes 9437184 | tf_op args[2]
  33.2 4.0 fusion.6
  39.4 4.4 %collective-permute-start.9 = (f32[1,128,256]{2,1,0:T(8,128)S(1)}, f32[1,128,256]{2,1,0:T(8,128)S(1)}, u32[]{:S(2)}, u32[]{:S(2)}) collective-permute-start(f32[1,128,256]{2,1,0:T(8,128)S(1)} %get-tuple-element.30), channel_id=1, source_target_pairs={{1,0},{2,1},{3,2},{4,3},{5,4},{6,5},{7,6},{8,7},{9,8},{10,9},{11,1... | collective-permute-start | bytes 393224 | tf_op jit(solution)/shard_map/ppermute | solution.py:19
  44.0 3.9 collective-permute-start.11
  60.1 3.8 multiply_reduce_fusion.3
  65.1 37.5 %all-reduce.1 = (f32[128,96]{0,1:T(8,128)S(1)}, f32[128]{0:T(128)}, f32[128]{0:T(128)}) all-reduce(f32[128,96]{0,1:T(8,128)} %fusion.53, f32[128]{0:T(128)} %get-tuple-element.4, f32[128]{0:T(128)} %get-tuple-element.3), channel_id=1, replica_groups=mesh['cluster'=2,'sub'=16] {'cluster','sub'}, use_global_device_ids=true, to_apply=%region_4.6 | all-reduce | flops 12544 | bytes 100352 | tf_op jit(solution)/shard_map/psum | solution.py:96
  103.4 41.8 %all-gather = f32[32,3,128]{2,1,0:T(4,128)S(1)} all-gather(f32[1,3,128]{2,1,0:T(4,128)S(1)} %convolution_bitcast_fusion.1), channel_id=1, replica_groups=mesh['cluster'=2,'sub'=16] {'cluster','sub'}, dimensions={0}, use_global_device_ids=true | all-gather | bytes 50688 | tf_op jit(solution)/shard_map/all_gather | solution.py:98
  155.5 4.5 %collective-permute-start.15 = (f32[1,128,256]{2,1,0:T(8,128)S(1)}, f32[1,128,256]{2,1,0:T(8,128)}, u32[]{:S(2)}, u32[]{:S(2)}) collective-permute-start(f32[1,128,256]{2,1,0:T(8,128)S(1)} %bitcast.568), channel_id=1, source_target_pairs={{1,0},{2,1},{3,2},{4,3},{5,4},{6,5},{7,6},{8,7},{9,8},{10,9},{11,1... | collective-permute-start | bytes 393224 | tf_op jit(solution)/shard_map/ppermute | solution.py:19
  162.1 4.0 collective-permute-start.17
  200.6 4.3 fusion.4
  207.7 4.4 %collective-permute-start.21 = (f32[1,128,256]{2,1,0:T(8,128)}, f32[1,128,256]{2,1,0:T(8,128)}, u32[]{:S(2)}, u32[]{:S(2)}) collective-permute-start(f32[1,128,256]{2,1,0:T(8,128)} %get-tuple-element.18), channel_id=1, source_target_pairs={{1,0},{2,1},{3,2},{4,3},{5,4},{6,5},{7,6},{8,7},{9,8},{10,9},{11,1... | collective-permute-start | bytes 393224 | tf_op jit(solution)/shard_map/ppermute | solution.py:19
  212.2 3.8 collective-permute-start.23
  253.5 36.9 %psum.45 = f32[128]{0:T(128)S(1)} all-reduce(f32[128]{0:T(128)S(1)} %multiply_reduce_fusion.1), channel_id=1, replica_groups=mesh['cluster'=2,'sub'=16] {'cluster','sub'}, use_global_device_ids=true, to_apply=%region_7.9 | all-reduce | flops 128 | bytes 1024 | tf_op jit(solution)/shard_map/psum | solution.py:82
  292.4 4.3 multiply_reduce_fusion
  297.0 41.7 %all-reduce = (f32[128]{0:T(128)}, f32[128,96]{0,1:T(8,128)S(1)}) all-reduce(f32[128]{0:T(128)} %get-tuple-element.85, f32[128,96]{0,1:T(8,128)S(1)} %fusion.52), channel_id=1, replica_groups=mesh['cluster'=2,'sub'=16] {'cluster','sub'}, use_global_device_ids=true, to_apply=%region_9.11 | all-reduce | flops 12416 | bytes 99328 | tf_op jit(solution)/shard_map/psum | solution.py:96
  338.8 41.1 %all-gather.1 = f32[32,3,128]{2,1,0:T(4,128)S(1)} all-gather(f32[1,3,128]{2,1,0:T(4,128)S(1)} %convolution_bitcast_fusion), channel_id=1, replica_groups=mesh['cluster'=2,'sub'=16] {'cluster','sub'}, dimensions={0}, use_global_device_ids=true | all-gather | bytes 50688 | tf_op jit(solution)/shard_map/all_gather | solution.py:98
  388.5 4.5 %collective-permute-start.27 = (f32[1,128,256]{2,1,0:T(8,128)S(1)}, f32[1,128,256]{2,1,0:T(8,128)}, u32[]{:S(2)}, u32[]{:S(2)}) collective-permute-start(f32[1,128,256]{2,1,0:T(8,128)S(1)} %bitcast.573), channel_id=1, source_target_pairs={{1,0},{2,1},{3,2},{4,3},{5,4},{6,5},{7,6},{8,7},{9,8},{10,9},{11,1... | collective-permute-start | bytes 393224 | tf_op jit(solution)/shard_map/ppermute | solution.py:19
  395.5 3.8 collective-permute-start.29
  416.1 2.8 bitcast_dynamic-update-slice_fusion.10
  418.9 2.7 bitcast_dynamic-update-slice_fusion.9
  428.3 3.8 multiply_subtract_fusion
  (397 shorter events, 153.9 us)
Async XLA Ops:
  5.4 18.9 %collective-permute-start.1 = (f32[1,128,256]{2,1,0:T(8,128)S(1)}, f32[1,128,256]{2,1,0:T(8,128)S(1)}, u32[]{:S(2)}, u32[]{:S(2)}) collective-permute-start(f32[1,128,256]{2,1,0:T(8,128)S(1)} %bitcast.564), channel_id=1, source_target_pairs={{16,0},{0,16},{17,1},{1,17},{18,2},{2,18},{19,3},{3,19},{20,4},{4,... | collective-permute-start | bytes 393224 | tf_op jit(solution)/shard_map/ppermute | solution.py:19
  5.6 19.7 %collective-permute-start.2 = (f32[1,128,256]{2,1,0:T(8,128)S(1)}, f32[1,128,256]{2,1,0:T(8,128)S(1)}, u32[]{:S(2)}, u32[]{:S(2)}) collective-permute-start(f32[1,128,256]{2,1,0:T(8,128)S(1)} %bitcast.560), channel_id=1, source_target_pairs={{0,1},{1,2},{2,3},{3,4},{4,5},{5,6},{6,7},{7,8},{8,9},{9,10},{10,1... | collective-permute-start | bytes 393224 | tf_op jit(solution)/shard_map/ppermute | solution.py:16
  5.8 20.5 %collective-permute-start.3 = (f32[1,128,256]{2,1,0:T(8,128)S(1)}, f32[1,128,256]{2,1,0:T(8,128)S(1)}, u32[]{:S(2)}, u32[]{:S(2)}) collective-permute-start(f32[1,128,256]{2,1,0:T(8,128)S(1)} %bitcast.561), channel_id=1, source_target_pairs={{1,0},{2,1},{3,2},{4,3},{5,4},{6,5},{7,6},{8,7},{9,8},{10,9},{11,1... | collective-permute-start | bytes 393224 | tf_op jit(solution)/shard_map/ppermute | solution.py:19
  10.4 16.9 %collective-permute-start.4 = (f32[128,256]{1,0:T(8,128)S(1)}, f32[128,256]{1,0:T(8,128)S(1)}, u32[]{:S(2)}, u32[]{:S(2)}) collective-permute-start(f32[128,256]{1,0:T(8,128)S(1)} %bitcast.559), channel_id=1, source_target_pairs={{0,4},{1,5},{2,6},{3,7},{4,8},{5,9},{6,10},{7,11},{8,12},{9,13},{1... | collective-permute-start | bytes 393224 | tf_op jit(solution)/shard_map/ppermute | solution.py:27
  12.5 15.7 %collective-permute-start.5 = (f32[128,256]{1,0:T(8,128)S(1)}, f32[128,256]{1,0:T(8,128)S(1)}, u32[]{:S(2)}, u32[]{:S(2)}) collective-permute-start(f32[128,256]{1,0:T(8,128)S(1)} %bitcast.562), channel_id=1, source_target_pairs={{0,12},{1,13},{2,14},{3,15},{4,0},{5,1},{6,2},{7,3},{8,4},{9,5},{1... | collective-permute-start | bytes 393224 | tf_op jit(solution)/shard_map/ppermute | solution.py:27
  39.4 10.4 %collective-permute-start.8 = (f32[1,128,256]{2,1,0:T(8,128)S(1)}, f32[1,128,256]{2,1,0:T(8,128)S(1)}, u32[]{:S(2)}, u32[]{:S(2)}) collective-permute-start(f32[1,128,256]{2,1,0:T(8,128)S(1)} %get-tuple-element.32), channel_id=1, source_target_pairs={{0,1},{1,2},{2,3},{3,4},{4,5},{5,6},{6,7},{7,8},{8,9},{9,10},{10,1... | collective-permute-start | bytes 393224 | tf_op jit(solution)/shard_map/ppermute | solution.py:16
  39.4 11.3 %collective-permute-start.9 = (f32[1,128,256]{2,1,0:T(8,128)S(1)}, f32[1,128,256]{2,1,0:T(8,128)S(1)}, u32[]{:S(2)}, u32[]{:S(2)}) collective-permute-start(f32[1,128,256]{2,1,0:T(8,128)S(1)} %get-tuple-element.30), channel_id=1, source_target_pairs={{1,0},{2,1},{3,2},{4,3},{5,4},{6,5},{7,6},{8,7},{9,8},{10,9},{11,1... | collective-permute-start | bytes 393224 | tf_op jit(solution)/shard_map/ppermute | solution.py:19
  151.1 11.0 %collective-permute-start.12 = (f32[1,128,256]{2,1,0:T(8,128)S(1)}, f32[1,128,256]{2,1,0:T(8,128)S(1)}, u32[]{:S(2)}, u32[]{:S(2)}) collective-permute-start(f32[1,128,256]{2,1,0:T(8,128)S(1)} %bitcast.569), channel_id=1, source_target_pairs={{0,16},{16,0},{1,17},{17,1},{2,18},{18,2},{3,19},{19,3},{4,20},{20... | collective-permute-start | bytes 393224 | tf_op jit(solution)/shard_map/ppermute | solution.py:16
  152.3 17.9 %collective-permute-start.13 = (f32[1,128,256]{2,1,0:T(8,128)S(1)}, f32[1,128,256]{2,1,0:T(8,128)}, u32[]{:S(2)}, u32[]{:S(2)}) collective-permute-start(f32[1,128,256]{2,1,0:T(8,128)S(1)} %bitcast.570), channel_id=1, source_target_pairs={{16,0},{0,16},{17,1},{1,17},{18,2},{2,18},{19,3},{3,19},{20,4},{4,... | collective-permute-start | bytes 393224 | tf_op jit(solution)/shard_map/ppermute | solution.py:19
  155.3 18.9 %collective-permute-start.14 = (f32[1,128,256]{2,1,0:T(8,128)S(1)}, f32[1,128,256]{2,1,0:T(8,128)}, u32[]{:S(2)}, u32[]{:S(2)}) collective-permute-start(f32[1,128,256]{2,1,0:T(8,128)S(1)} %bitcast.567), channel_id=1, source_target_pairs={{0,1},{1,2},{2,3},{3,4},{4,5},{5,6},{6,7},{7,8},{8,9},{9,10},{10,1... | collective-permute-start | bytes 393224 | tf_op jit(solution)/shard_map/ppermute | solution.py:16
  155.5 22.7 %collective-permute-start.15 = (f32[1,128,256]{2,1,0:T(8,128)S(1)}, f32[1,128,256]{2,1,0:T(8,128)}, u32[]{:S(2)}, u32[]{:S(2)}) collective-permute-start(f32[1,128,256]{2,1,0:T(8,128)S(1)} %bitcast.568), channel_id=1, source_target_pairs={{1,0},{2,1},{3,2},{4,3},{5,4},{6,5},{7,6},{8,7},{9,8},{10,9},{11,1... | collective-permute-start | bytes 393224 | tf_op jit(solution)/shard_map/ppermute | solution.py:19
  161.0 21.3 %collective-permute-start.16 = (f32[128,256]{1,0:T(8,128)S(1)}, f32[128,256]{1,0:T(8,128)}, u32[]{:S(2)}, u32[]{:S(2)}) collective-permute-start(f32[128,256]{1,0:T(8,128)S(1)} %bitcast.565), channel_id=1, source_target_pairs={{0,4},{1,5},{2,6},{3,7},{4,8},{5,9},{6,10},{7,11},{8,12},{9,13},{1... | collective-permute-start | bytes 393224 | tf_op jit(solution)/shard_map/ppermute | solution.py:27
  162.1 25.8 %collective-permute-start.17 = (f32[128,256]{1,0:T(8,128)S(1)}, f32[128,256]{1,0:T(8,128)}, u32[]{:S(2)}, u32[]{:S(2)}) collective-permute-start(f32[128,256]{1,0:T(8,128)S(1)} %bitcast.566), channel_id=1, source_target_pairs={{0,12},{1,13},{2,14},{3,15},{4,0},{5,1},{6,2},{7,3},{8,4},{9,5},{1... | collective-permute-start | bytes 393224 | tf_op jit(solution)/shard_map/ppermute | solution.py:27
  205.8 14.2 %collective-permute-start.19 = (f32[1,128,256]{2,1,0:T(8,128)}, f32[1,128,256]{2,1,0:T(8,128)}, u32[]{:S(2)}, u32[]{:S(2)}) collective-permute-start(f32[1,128,256]{2,1,0:T(8,128)} %get-tuple-element.17), channel_id=1, source_target_pairs={{16,0},{0,16},{17,1},{1,17},{18,2},{2,18},{19,3},{3,19},{20,4},{4,... | collective-permute-start | bytes 393224 | tf_op jit(solution)/shard_map/ppermute | solution.py:19
  207.7 16.3 %collective-permute-start.20 = (f32[1,128,256]{2,1,0:T(8,128)}, f32[1,128,256]{2,1,0:T(8,128)}, u32[]{:S(2)}, u32[]{:S(2)}) collective-permute-start(f32[1,128,256]{2,1,0:T(8,128)} %get-tuple-element.20), channel_id=1, source_target_pairs={{0,1},{1,2},{2,3},{3,4},{4,5},{5,6},{6,7},{7,8},{8,9},{9,10},{10,1... | collective-permute-start | bytes 393224 | tf_op jit(solution)/shard_map/ppermute | solution.py:16
  207.7 20.3 %collective-permute-start.21 = (f32[1,128,256]{2,1,0:T(8,128)}, f32[1,128,256]{2,1,0:T(8,128)}, u32[]{:S(2)}, u32[]{:S(2)}) collective-permute-start(f32[1,128,256]{2,1,0:T(8,128)} %get-tuple-element.18), channel_id=1, source_target_pairs={{1,0},{2,1},{3,2},{4,3},{5,4},{6,5},{7,6},{8,7},{9,8},{10,9},{11,1... | collective-permute-start | bytes 393224 | tf_op jit(solution)/shard_map/ppermute | solution.py:19
  212.2 19.9 %collective-permute-start.22 = (f32[128,256]{1,0:T(8,128)}, f32[128,256]{1,0:T(8,128)}, u32[]{:S(2)}, u32[]{:S(2)}) collective-permute-start(f32[128,256]{1,0:T(8,128)} %get-tuple-element.19), channel_id=1, source_target_pairs={{0,4},{1,5},{2,6},{3,7},{4,8},{5,9},{6,10},{7,11},{8,12},{9,13},{1... | collective-permute-start | bytes 393224 | tf_op jit(solution)/shard_map/ppermute | solution.py:27
  212.2 26.1 %collective-permute-start.23 = (f32[128,256]{1,0:T(8,128)}, f32[128,256]{1,0:T(8,128)}, u32[]{:S(2)}, u32[]{:S(2)}) collective-permute-start(f32[128,256]{1,0:T(8,128)} %get-tuple-element.16), channel_id=1, source_target_pairs={{0,12},{1,13},{2,14},{3,15},{4,0},{5,1},{6,2},{7,3},{8,4},{9,5},{1... | collective-permute-start | bytes 393224 | tf_op jit(solution)/shard_map/ppermute | solution.py:27
  383.2 12.3 %collective-permute-start.24 = (f32[1,128,256]{2,1,0:T(8,128)S(1)}, f32[1,128,256]{2,1,0:T(8,128)S(1)}, u32[]{:S(2)}, u32[]{:S(2)}) collective-permute-start(f32[1,128,256]{2,1,0:T(8,128)S(1)} %bitcast.574), channel_id=1, source_target_pairs={{0,16},{16,0},{1,17},{17,1},{2,18},{18,2},{3,19},{19,3},{4,20},{20... | collective-permute-start | bytes 393224 | tf_op jit(solution)/shard_map/ppermute | solution.py:16
  384.5 17.3 %collective-permute-start.25 = (f32[1,128,256]{2,1,0:T(8,128)S(1)}, f32[1,128,256]{2,1,0:T(8,128)}, u32[]{:S(2)}, u32[]{:S(2)}) collective-permute-start(f32[1,128,256]{2,1,0:T(8,128)S(1)} %bitcast.575), channel_id=1, source_target_pairs={{16,0},{0,16},{17,1},{1,17},{18,2},{2,18},{19,3},{3,19},{20,4},{4,... | collective-permute-start | bytes 393224 | tf_op jit(solution)/shard_map/ppermute | solution.py:19
  387.4 17.0 %collective-permute-start.26 = (f32[1,128,256]{2,1,0:T(8,128)S(1)}, f32[1,128,256]{2,1,0:T(8,128)}, u32[]{:S(2)}, u32[]{:S(2)}) collective-permute-start(f32[1,128,256]{2,1,0:T(8,128)S(1)} %bitcast.572), channel_id=1, source_target_pairs={{0,1},{1,2},{2,3},{3,4},{4,5},{5,6},{6,7},{7,8},{8,9},{9,10},{10,1... | collective-permute-start | bytes 393224 | tf_op jit(solution)/shard_map/ppermute | solution.py:16
  388.5 18.4 %collective-permute-start.27 = (f32[1,128,256]{2,1,0:T(8,128)S(1)}, f32[1,128,256]{2,1,0:T(8,128)}, u32[]{:S(2)}, u32[]{:S(2)}) collective-permute-start(f32[1,128,256]{2,1,0:T(8,128)S(1)} %bitcast.573), channel_id=1, source_target_pairs={{1,0},{2,1},{3,2},{4,3},{5,4},{6,5},{7,6},{8,7},{9,8},{10,9},{11,1... | collective-permute-start | bytes 393224 | tf_op jit(solution)/shard_map/ppermute | solution.py:19
  394.0 15.5 %collective-permute-start.28 = (f32[128,256]{1,0:T(8,128)S(1)}, f32[128,256]{1,0:T(8,128)}, u32[]{:S(2)}, u32[]{:S(2)}) collective-permute-start(f32[128,256]{1,0:T(8,128)S(1)} %bitcast.571), channel_id=1, source_target_pairs={{0,4},{1,5},{2,6},{3,7},{4,8},{5,9},{6,10},{7,11},{8,12},{9,13},{1... | collective-permute-start | bytes 393224 | tf_op jit(solution)/shard_map/ppermute | solution.py:27
  395.5 16.5 %collective-permute-start.29 = (f32[128,256]{1,0:T(8,128)}, f32[128,256]{1,0:T(8,128)}, u32[]{:S(2)}, u32[]{:S(2)}) collective-permute-start(f32[128,256]{1,0:T(8,128)} %bitcast.155), channel_id=1, source_target_pairs={{0,12},{1,13},{2,14},{3,15},{4,0},{5,1},{6,2},{7,3},{8,4},{9,5},{1... | collective-permute-start | bytes 393224 | tf_op jit(solution)/shard_map/ppermute | solution.py:27
  (87 other events, 1831.1 us)
where the time goes:
time: 434 us; the launch traced here: 432 us
  blocking collectives  199 us (46%)
  local copies, waits for them, and re-layouts  101 us (23%)
  starting transfers between devices  53.7 us (12%)
  other arithmetic  53 us (12%)
  matrix products  23.3 us (5%)
    all_gather x2, blocking collectives, local(): lax.all_gather(own_values, ('cluster', 'sub'), axis=1, tiled=True)  82.9 us
    psum x2, blocking collectives, local(): lax.psum((coarse_local, local_curve), ('cluster', 'sub'))  79.2 us
    gather x60, local copies, waits for them, and re-layouts, assemble(): permuted = jnp.take(received[face_index], slot_maps[face_index], axis=1)  55.5 us
    unnamed x25, other arithmetic  39.7 us
    psum x1, blocking collectives, precond_with_product(): lax.psum(jnp.sum(vector * precond, axis=1), ('cluster', 'sub'))  36.9 us
    ppermute x10, starting transfers between devices, padded(): lax.ppermute(lax.slice_in_dim(block, 0, width, axis=dim), axis, backward)  28.2 us
    unnamed x184, local copies, waits for them, and re-layouts  20.4 us
    ppermute x10, starting transfers between devices, passed_along(): return lax.ppermute(value, axis, pairs)  19.6 us
  transfers between devices with their start and end apart: 30, of which 0 were waited for; matrix products, arithmetic and copies ran while one was open for 20% of the time, Pallas kernels for 0%

commit v1 on v0

--- a/solution.py
+++ b/solution.py
@@ -79,7 +79,9 @@
             vector.astype(jnp.bfloat16), precond_local, preferred_element_type=jnp.float32
         )
         precond = assemble(local_term)
-        product = 0.5 * lax.psum(jnp.sum(vector * precond, axis=1), ("cluster", "sub"))
+        product = 0.5 * jnp.sum(
+            lax.all_gather(jnp.sum(vector * precond, axis=1), ("cluster", "sub")), axis=0
+        )
         return (precond, product)
 
     right_side = assemble(local_loads)

time: 434 us -> 469 us (1.081)
  blocking collectives: 199 us -> 232 us
    all_gather x0 -> x2, blocking collectives: none -> 73.2 us  [precond_with_product(): lax.all_gather(jnp.sum(vector * precond, axis=1), ('cluster', 'sub'))]
    psum x1 -> x0, blocking collectives: 36.9 us -> none  [precond_with_product(): lax.psum(jnp.sum(vector * precond, axis=1), ('cluster', 'sub'))]
    unnamed x184 -> x182, local copies, waits for them, and re-layouts: 20.4 us -> 20.4 us
  transfers between devices with their start and end apart: 30 -> 30, of which waited for: 0 -> 0; matrix products, arithmetic and copies ran while one was open for 20% -> 18% of each run, Pallas kernels for 0% -> 0%
where the time goes in v1:
time: 469 us; the launch traced here: 467 us
  blocking collectives  232 us (49%)
  local copies, waits for them, and re-layouts  102 us (22%)
  starting transfers between devices  53.8 us (11%)
  other arithmetic  52.6 us (11%)
  matrix products  23.7 us (5%)
    all_gather x2, blocking collectives, local(): lax.all_gather(own_values, ('cluster', 'sub'), axis=1, tiled=True)  83.1 us
    psum x2, blocking collectives, local(): lax.psum((coarse_local, local_curve), ('cluster', 'sub'))  75.7 us
    all_gather x2, blocking collectives, precond_with_product(): lax.all_gather(jnp.sum(vector * precond, axis=1), ('cluster', 'sub'))  73.2 us
    gather x60, local copies, waits for them, and re-layouts, assemble(): permuted = jnp.take(received[face_index], slot_maps[face_index], axis=1)  55.4 us
    unnamed x25, other arithmetic  39.8 us
    ppermute x10, starting transfers between devices, padded(): lax.ppermute(lax.slice_in_dim(block, 0, width, axis=dim), axis, backward)  28.1 us
    unnamed x182, local copies, waits for them, and re-layouts  20.4 us
    ppermute x10, starting transfers between devices, passed_along(): return lax.ppermute(value, axis, pairs)  19.9 us
  transfers between devices with their start and end apart: 30, of which 0 were waited for; matrix products, arithmetic and copies ran while one was open for 18% of the time, Pallas kernels for 0%

profile of v1, /device:TPU:0, one launch (start us, length us, event | category | flops | bytes accessed | tf_op | source)
XLA Modules:
  0.0 466.9 jit_solution(3545503340673559215)
XLA Ops:
  2.3 3.0 collective-permute-start
  5.8 4.5 collective-permute-start.3
  12.5 3.6 collective-permute-start.5
  16.1 6.7 %copy.173 = bf16[1,1536,1536]{1,2,0:T(8,128)(2,1)} copy(bf16[1,1536,1536]{2,1,0:T(8,128)(2,1)} %param.12) | data formatting | bytes 9437184 | tf_op args[2]
  33.1 4.0 fusion.6
  39.9 4.4 collective-permute-start.9
  44.5 3.9 collective-permute-start.11
  60.5 3.8 multiply_reduce_fusion.3
  65.5 37.8 %all-reduce.1 = (f32[128,96]{0,1:T(8,128)S(1)}, f32[128]{0:T(128)}) all-reduce(f32[128,96]{0,1:T(8,128)} %fusion.53, f32[128]{0:T(128)} %get-tuple-element.4), channel_id=1, replica_groups=mesh['cluster'=2,'sub'=16] {'cluster','sub'}, use_global_device_ids=true, to_apply=%region_4.6 | all-reduce | flops 12416 | bytes 99328 | tf_op jit(solution)/shard_map/psum | solution.py:98
  104.1 41.4 %all-gather.3 = f32[32,3,128]{2,1,0:T(4,128)S(1)} all-gather(f32[1,3,128]{2,1,0:T(4,128)S(1)} %convolution_bitcast_fusion.1), channel_id=1, replica_groups=mesh['cluster'=2,'sub'=16] {'cluster','sub'}, dimensions={0}, use_global_device_ids=true | all-gather | bytes 50688 | tf_op jit(solution)/shard_map/all_gather | solution.py:100
  147.0 36.9 %all-gather.2 = f32[32,1,128]{2,1,0:T(1,128)S(1)} all-gather(f32[1,1,128]{2,1,0:T(1,128)} %bitcast.602), channel_id=2, replica_groups=mesh['cluster'=2,'sub'=16] {'cluster','sub'}, dimensions={0}, use_global_device_ids=true | all-gather | bytes 16896 | tf_op jit(solution)/shard_map/all_gather | solution.py:83
  192.6 4.5 collective-permute-start.15
  199.3 4.0 collective-permute-start.17
  237.7 4.3 fusion.4
  244.8 4.4 collective-permute-start.21
  249.2 3.8 collective-permute-start.23
  290.4 36.4 %all-gather.4 = f32[32,1,128]{2,1,0:T(1,128)S(1)} all-gather(f32[1,1,128]{2,1,0:T(1,128)S(1)} %bitcast.601), channel_id=3, replica_groups=mesh['cluster'=2,'sub'=16] {'cluster','sub'}, dimensions={0}, use_global_device_ids=true | all-gather | bytes 16896 | tf_op jit(solution)/shard_map/all_gather | solution.py:83
  328.8 4.3 multiply_reduce_fusion
  334.0 37.9 %all-reduce = (f32[128]{0:T(128)}, f32[128,96]{0,1:T(8,128)S(1)}) all-reduce(f32[128]{0:T(128)} %get-tuple-element.84, f32[128,96]{0,1:T(8,128)S(1)} %fusion.52), channel_id=1, replica_groups=mesh['cluster'=2,'sub'=16] {'cluster','sub'}, use_global_device_ids=true, to_apply=%region_9.11 | all-reduce | flops 12416 | bytes 99328 | tf_op jit(solution)/shard_map/psum | solution.py:98
  372.1 41.6 %all-gather.5 = f32[32,3,128]{2,1,0:T(4,128)S(1)} all-gather(f32[1,3,128]{2,1,0:T(4,128)S(1)} %convolution_bitcast_fusion), channel_id=1, replica_groups=mesh['cluster'=2,'sub'=16] {'cluster','sub'}, dimensions={0}, use_global_device_ids=true | all-gather | bytes 50688 | tf_op jit(solution)/shard_map/all_gather | solution.py:100
  422.2 4.5 collective-permute-start.27
  429.2 4.1 collective-permute-start.29
  451.0 2.8 bitcast_dynamic-update-slice_fusion.10
  463.1 3.8 multiply_subtract_fusion
  (398 shorter events, 158.1 us)
Async XLA Ops:
  5.4 19.0 %collective-permute-start.1 = (f32[1,128,256]{2,1,0:T(8,128)S(1)}, f32[1,128,256]{2,1,0:T(8,128)S(1)}, u32[]{:S(2)}, u32[]{:S(2)}) collective-permute-start(f32[1,128,256]{2,1,0:T(8,128)S(1)} %bitcast.566), channel_id=1, source_target_pairs={{16,0},{0,16},{17,1},{1,17},{18,2},{2,18},{19,3},{3,19},{20,4},{4,... | collective-permute-start | bytes 393224 | tf_op jit(solution)/shard_map/ppermute | solution.py:19
  5.6 19.7 %collective-permute-start.2 = (f32[1,128,256]{2,1,0:T(8,128)S(1)}, f32[1,128,256]{2,1,0:T(8,128)S(1)}, u32[]{:S(2)}, u32[]{:S(2)}) collective-permute-start(f32[1,128,256]{2,1,0:T(8,128)S(1)} %bitcast.562), channel_id=1, source_target_pairs={{0,1},{1,2},{2,3},{3,4},{4,5},{5,6},{6,7},{7,8},{8,9},{9,10},{10,1... | collective-permute-start | bytes 393224 | tf_op jit(solution)/shard_map/ppermute | solution.py:16
  5.8 20.5 %collective-permute-start.3 = (f32[1,128,256]{2,1,0:T(8,128)S(1)}, f32[1,128,256]{2,1,0:T(8,128)S(1)}, u32[]{:S(2)}, u32[]{:S(2)}) collective-permute-start(f32[1,128,256]{2,1,0:T(8,128)S(1)} %bitcast.563), channel_id=1, source_target_pairs={{1,0},{2,1},{3,2},{4,3},{5,4},{6,5},{7,6},{8,7},{9,8},{10,9},{11,1... | collective-permute-start | bytes 393224 | tf_op jit(solution)/shard_map/ppermute | solution.py:19
  10.4 16.9 %collective-permute-start.4 = (f32[128,256]{1,0:T(8,128)S(1)}, f32[128,256]{1,0:T(8,128)S(1)}, u32[]{:S(2)}, u32[]{:S(2)}) collective-permute-start(f32[128,256]{1,0:T(8,128)S(1)} %bitcast.561), channel_id=1, source_target_pairs={{0,4},{1,5},{2,6},{3,7},{4,8},{5,9},{6,10},{7,11},{8,12},{9,13},{1... | collective-permute-start | bytes 393224 | tf_op jit(solution)/shard_map/ppermute | solution.py:27
  12.5 15.7 %collective-permute-start.5 = (f32[128,256]{1,0:T(8,128)S(1)}, f32[128,256]{1,0:T(8,128)S(1)}, u32[]{:S(2)}, u32[]{:S(2)}) collective-permute-start(f32[128,256]{1,0:T(8,128)S(1)} %bitcast.564), channel_id=1, source_target_pairs={{0,12},{1,13},{2,14},{3,15},{4,0},{5,1},{6,2},{7,3},{8,4},{9,5},{1... | collective-permute-start | bytes 393224 | tf_op jit(solution)/shard_map/ppermute | solution.py:27
  39.9 10.4 %collective-permute-start.8 = (f32[1,128,256]{2,1,0:T(8,128)S(1)}, f32[1,128,256]{2,1,0:T(8,128)S(1)}, u32[]{:S(2)}, u32[]{:S(2)}) collective-permute-start(f32[1,128,256]{2,1,0:T(8,128)S(1)} %get-tuple-element.31), channel_id=1, source_target_pairs={{0,1},{1,2},{2,3},{3,4},{4,5},{5,6},{6,7},{7,8},{8,9},{9,10},{10,1... | collective-permute-start | bytes 393224 | tf_op jit(solution)/shard_map/ppermute | solution.py:16
  39.9 11.3 %collective-permute-start.9 = (f32[1,128,256]{2,1,0:T(8,128)S(1)}, f32[1,128,256]{2,1,0:T(8,128)S(1)}, u32[]{:S(2)}, u32[]{:S(2)}) collective-permute-start(f32[1,128,256]{2,1,0:T(8,128)S(1)} %get-tuple-element.29), channel_id=1, source_target_pairs={{1,0},{2,1},{3,2},{4,3},{5,4},{6,5},{7,6},{8,7},{9,8},{10,9},{11,1... | collective-permute-start | bytes 393224 | tf_op jit(solution)/shard_map/ppermute | solution.py:19
  188.3 11.0 %collective-permute-start.12 = (f32[1,128,256]{2,1,0:T(8,128)S(1)}, f32[1,128,256]{2,1,0:T(8,128)S(1)}, u32[]{:S(2)}, u32[]{:S(2)}) collective-permute-start(f32[1,128,256]{2,1,0:T(8,128)S(1)} %bitcast.571), channel_id=1, source_target_pairs={{0,16},{16,0},{1,17},{17,1},{2,18},{18,2},{3,19},{19,3},{4,20},{20... | collective-permute-start | bytes 393224 | tf_op jit(solution)/shard_map/ppermute | solution.py:16
  189.4 18.0 %collective-permute-start.13 = (f32[1,128,256]{2,1,0:T(8,128)S(1)}, f32[1,128,256]{2,1,0:T(8,128)}, u32[]{:S(2)}, u32[]{:S(2)}) collective-permute-start(f32[1,128,256]{2,1,0:T(8,128)S(1)} %bitcast.572), channel_id=1, source_target_pairs={{16,0},{0,16},{17,1},{1,17},{18,2},{2,18},{19,3},{3,19},{20,4},{4,... | collective-permute-start | bytes 393224 | tf_op jit(solution)/shard_map/ppermute | solution.py:19
  192.5 18.9 %collective-permute-start.14 = (f32[1,128,256]{2,1,0:T(8,128)S(1)}, f32[1,128,256]{2,1,0:T(8,128)}, u32[]{:S(2)}, u32[]{:S(2)}) collective-permute-start(f32[1,128,256]{2,1,0:T(8,128)S(1)} %bitcast.569), channel_id=1, source_target_pairs={{0,1},{1,2},{2,3},{3,4},{4,5},{5,6},{6,7},{7,8},{8,9},{9,10},{10,1... | collective-permute-start | bytes 393224 | tf_op jit(solution)/shard_map/ppermute | solution.py:16
  192.6 22.8 %collective-permute-start.15 = (f32[1,128,256]{2,1,0:T(8,128)S(1)}, f32[1,128,256]{2,1,0:T(8,128)}, u32[]{:S(2)}, u32[]{:S(2)}) collective-permute-start(f32[1,128,256]{2,1,0:T(8,128)S(1)} %bitcast.570), channel_id=1, source_target_pairs={{1,0},{2,1},{3,2},{4,3},{5,4},{6,5},{7,6},{8,7},{9,8},{10,9},{11,1... | collective-permute-start | bytes 393224 | tf_op jit(solution)/shard_map/ppermute | solution.py:19
  198.1 21.3 %collective-permute-start.16 = (f32[128,256]{1,0:T(8,128)S(1)}, f32[128,256]{1,0:T(8,128)}, u32[]{:S(2)}, u32[]{:S(2)}) collective-permute-start(f32[128,256]{1,0:T(8,128)S(1)} %bitcast.567), channel_id=1, source_target_pairs={{0,4},{1,5},{2,6},{3,7},{4,8},{5,9},{6,10},{7,11},{8,12},{9,13},{1... | collective-permute-start | bytes 393224 | tf_op jit(solution)/shard_map/ppermute | solution.py:27
  199.3 25.8 %collective-permute-start.17 = (f32[128,256]{1,0:T(8,128)S(1)}, f32[128,256]{1,0:T(8,128)}, u32[]{:S(2)}, u32[]{:S(2)}) collective-permute-start(f32[128,256]{1,0:T(8,128)S(1)} %bitcast.568), channel_id=1, source_target_pairs={{0,12},{1,13},{2,14},{3,15},{4,0},{5,1},{6,2},{7,3},{8,4},{9,5},{1... | collective-permute-start | bytes 393224 | tf_op jit(solution)/shard_map/ppermute | solution.py:27
  242.8 14.3 %collective-permute-start.19 = (f32[1,128,256]{2,1,0:T(8,128)}, f32[1,128,256]{2,1,0:T(8,128)}, u32[]{:S(2)}, u32[]{:S(2)}) collective-permute-start(f32[1,128,256]{2,1,0:T(8,128)} %get-tuple-element.16), channel_id=1, source_target_pairs={{16,0},{0,16},{17,1},{1,17},{18,2},{2,18},{19,3},{3,19},{20,4},{4,... | collective-permute-start | bytes 393224 | tf_op jit(solution)/shard_map/ppermute | solution.py:19
  244.8 16.3 %collective-permute-start.20 = (f32[1,128,256]{2,1,0:T(8,128)}, f32[1,128,256]{2,1,0:T(8,128)}, u32[]{:S(2)}, u32[]{:S(2)}) collective-permute-start(f32[1,128,256]{2,1,0:T(8,128)} %get-tuple-element.19), channel_id=1, source_target_pairs={{0,1},{1,2},{2,3},{3,4},{4,5},{5,6},{6,7},{7,8},{8,9},{9,10},{10,1... | collective-permute-start | bytes 393224 | tf_op jit(solution)/shard_map/ppermute | solution.py:16
  244.8 20.3 %collective-permute-start.21 = (f32[1,128,256]{2,1,0:T(8,128)}, f32[1,128,256]{2,1,0:T(8,128)}, u32[]{:S(2)}, u32[]{:S(2)}) collective-permute-start(f32[1,128,256]{2,1,0:T(8,128)} %get-tuple-element.17), channel_id=1, source_target_pairs={{1,0},{2,1},{3,2},{4,3},{5,4},{6,5},{7,6},{8,7},{9,8},{10,9},{11,1... | collective-permute-start | bytes 393224 | tf_op jit(solution)/shard_map/ppermute | solution.py:19
  249.2 19.9 %collective-permute-start.22 = (f32[128,256]{1,0:T(8,128)}, f32[128,256]{1,0:T(8,128)}, u32[]{:S(2)}, u32[]{:S(2)}) collective-permute-start(f32[128,256]{1,0:T(8,128)} %get-tuple-element.18), channel_id=1, source_target_pairs={{0,4},{1,5},{2,6},{3,7},{4,8},{5,9},{6,10},{7,11},{8,12},{9,13},{1... | collective-permute-start | bytes 393224 | tf_op jit(solution)/shard_map/ppermute | solution.py:27
  249.2 26.1 %collective-permute-start.23 = (f32[128,256]{1,0:T(8,128)}, f32[128,256]{1,0:T(8,128)}, u32[]{:S(2)}, u32[]{:S(2)}) collective-permute-start(f32[128,256]{1,0:T(8,128)} %get-tuple-element.15), channel_id=1, source_target_pairs={{0,12},{1,13},{2,14},{3,15},{4,0},{5,1},{6,2},{7,3},{8,4},{9,5},{1... | collective-permute-start | bytes 393224 | tf_op jit(solution)/shard_map/ppermute | solution.py:27
  417.0 12.2 %collective-permute-start.24 = (f32[1,128,256]{2,1,0:T(8,128)S(1)}, f32[1,128,256]{2,1,0:T(8,128)S(1)}, u32[]{:S(2)}, u32[]{:S(2)}) collective-permute-start(f32[1,128,256]{2,1,0:T(8,128)S(1)} %bitcast.576), channel_id=1, source_target_pairs={{0,16},{16,0},{1,17},{17,1},{2,18},{18,2},{3,19},{19,3},{4,20},{20... | collective-permute-start | bytes 393224 | tf_op jit(solution)/shard_map/ppermute | solution.py:16
  418.5 18.3 %collective-permute-start.25 = (f32[1,128,256]{2,1,0:T(8,128)S(1)}, f32[1,128,256]{2,1,0:T(8,128)}, u32[]{:S(2)}, u32[]{:S(2)}) collective-permute-start(f32[1,128,256]{2,1,0:T(8,128)S(1)} %bitcast.577), channel_id=1, source_target_pairs={{16,0},{0,16},{17,1},{1,17},{18,2},{2,18},{19,3},{3,19},{20,4},{4,... | collective-permute-start | bytes 393224 | tf_op jit(solution)/shard_map/ppermute | solution.py:19
  421.2 18.1 %collective-permute-start.26 = (f32[1,128,256]{2,1,0:T(8,128)S(1)}, f32[1,128,256]{2,1,0:T(8,128)}, u32[]{:S(2)}, u32[]{:S(2)}) collective-permute-start(f32[1,128,256]{2,1,0:T(8,128)S(1)} %bitcast.574), channel_id=1, source_target_pairs={{0,1},{1,2},{2,3},{3,4},{4,5},{5,6},{6,7},{7,8},{8,9},{9,10},{10,1... | collective-permute-start | bytes 393224 | tf_op jit(solution)/shard_map/ppermute | solution.py:16
  422.2 19.6 %collective-permute-start.27 = (f32[1,128,256]{2,1,0:T(8,128)S(1)}, f32[1,128,256]{2,1,0:T(8,128)}, u32[]{:S(2)}, u32[]{:S(2)}) collective-permute-start(f32[1,128,256]{2,1,0:T(8,128)S(1)} %bitcast.575), channel_id=1, source_target_pairs={{1,0},{2,1},{3,2},{4,3},{5,4},{6,5},{7,6},{8,7},{9,8},{10,9},{11,1... | collective-permute-start | bytes 393224 | tf_op jit(solution)/shard_map/ppermute | solution.py:19
  427.7 16.6 %collective-permute-start.28 = (f32[128,256]{1,0:T(8,128)S(1)}, f32[128,256]{1,0:T(8,128)}, u32[]{:S(2)}, u32[]{:S(2)}) collective-permute-start(f32[128,256]{1,0:T(8,128)S(1)} %bitcast.573), channel_id=1, source_target_pairs={{0,4},{1,5},{2,6},{3,7},{4,8},{5,9},{6,10},{7,11},{8,12},{9,13},{1... | collective-permute-start | bytes 393224 | tf_op jit(solution)/shard_map/ppermute | solution.py:27
  429.2 17.7 %collective-permute-start.29 = (f32[128,256]{1,0:T(8,128)}, f32[128,256]{1,0:T(8,128)}, u32[]{:S(2)}, u32[]{:S(2)}) collective-permute-start(f32[128,256]{1,0:T(8,128)} %bitcast.157), channel_id=1, source_target_pairs={{0,12},{1,13},{2,14},{3,15},{4,0},{5,1},{6,2},{7,3},{8,4},{9,5},{1... | collective-permute-start | bytes 393224 | tf_op jit(solution)/shard_map/ppermute | solution.py:27
  (86 other events, 1900.8 us)
